TPU v7x, 32 devices: a whole 2x2x4 slice. The times are simulated.
32 devices in a mesh: edge: 8 (over y, x, core), feat: 4 (over z).
Axes of the slice: x: 2, y: 2, z: 4, core: 2. Of those that a mesh axis runs over, the one named last changes fastest.
Arguments:
- node_latents: bfloat16 [4, 4096, 256], P('feat', 'edge'), may hold values from -6 to 6
- edge_latents: bfloat16 [4, 32768, 256], P('feat', 'edge'), may hold values from -6 to 6
- senders: int32 [32768], P('edge'), may hold values from 0 to 4095, as said below
- receivers: int32 [32768], P('edge'), may hold values from 0 to 4095, as said below
- regions: int32 [32768], P('edge'), may hold values from 0 to 23
- forced: int32 [4096], P('edge'), may hold values 0 or 1
- params: float32 [1824, 256], P('feat'), may hold values from -1.5 to 1.5, as said below
- first_moment: float32 [1824, 256], P('feat'), may hold values from -0.34 to 0.34
- second_moment: float32 [1824, 256], P('feat'), may hold values from 0.004 to 0.22
- averaged: float32 [1824, 256], P('feat'), may hold values from -1.7 to 1.7
- step: int32 [1], replicated, may hold values from 1 to 20
- cotangent: float32 [4, 4096, 256], P('feat', 'edge'), may hold values from -6 to 6
Outputs:
- new_latents: float32 [4, 4096, 256], P('feat', 'edge')
- grad_latents: float32 [4, 4096, 256], P('feat', 'edge')
- grad_edges: bfloat16 [4, 32768, 256], P('feat', 'edge')
- new_first: float32 [1824, 256], P('feat')
- new_second: float32 [1824, 256], P('feat')
- new_params: float32 [1824, 256], P('feat')
- new_average: float32 [1824, 256], P('feat')
- grad_norm: float32 [1], replicated
- vector_grads: float32 [8, 256], replicated
Inputs may be any that keep to these rules, and one draw needn't show every extreme that they name: `senders`: nodes are numbered so that node block b is nodes b * 512 to (b + 1) * 512 - 1. Edge k lies in edge block e = k // 4096; its sender lies in node block e - 1, e or e + 1, taken cyclically over the 4096 nodes. `receivers`: the receiver of edge k lies in node block e - 1, e or e + 1 of its edge block e = k // 4096, taken cyclically. `params`: parameters scaled by fan-in; gains near one.
All inputs are finite; a program needn't handle non-finite values. No bound on the sum of `forced` on one device may be relied on, other than what follows from the above.
Results may differ from a plain program's by a relative error of at most 0.0039.
The roundings to bfloat16 on the way count: a program that leaves them out, or rounds other values in their place, can miss the bound.
Values may be sent and summed in bfloat16 or wider, within the bound.
No kernel may reach another device: no remote copies, remote signals or barrier semaphores. Data moves between devices by JAX's collectives and lax.ppermute only.
A program may use at most 128 MiB of HBM per device.

v0:
```python
import jax
import jax.numpy as jnp
from jax import lax
from jax.sharding import PartitionSpec as P

NORM_EPS = 1e-05
MAX_NORM = 512.0
RATE = 0.05
BETA_ONE = 0.9
BETA_TWO = 0.95
ADAM_EPS = 1e-08
WEIGHT_DECAY = 0.1
AVERAGE_DECAY = 0.999


def padded(cells, sides, width):
    for axis, dim in sides:
        count = lax.axis_size(axis)
        head = lax.slice_in_dim(cells, 0, width, axis=dim)
        tail = lax.slice_in_dim(cells, cells.shape[dim] - width, cells.shape[dim], axis=dim)
        cells = jnp.concatenate(
            [
                lax.ppermute(tail, axis, [(i, (i + 1) % count) for i in range(count)]),
                cells,
                lax.ppermute(head, axis, [((i + 1) % count, i) for i in range(count)]),
            ],
            axis=dim,
        )
    return cells


def passed_along(value, axis, steps):
    count = lax.axis_size(axis)
    pairs = [(source, (source + steps) % count) for source in range(count)]
    return lax.ppermute(value, axis, pairs)


def product(left, right):
    return jnp.dot(left, right, preferred_element_type=jnp.float32)


def outer_product(left, right):
    return lax.dot_general(
        left, right, (((0,), (0,)), ((), ())), preferred_element_type=jnp.float32
    )


def product_transposed(left, right):
    return lax.dot_general(
        left, right, (((1,), (1,)), ((), ())), preferred_element_type=jnp.float32
    )


def pick_rows(table, indices):
    return jnp.take(table, indices, axis=0)


def add_rows(values, indices, rows):
    return jax.ops.segment_sum(values, indices, num_segments=rows)


def normalized(values):
    center = values - jnp.mean(values, axis=-1, keepdims=True)
    spread = jnp.mean(center * center, axis=-1, keepdims=True)
    inverse = lax.rsqrt(spread + NORM_EPS)
    return (center * inverse, inverse)


def layer_norm(values, gain, shift):
    unit, inverse = normalized(values)
    return unit * gain + shift


def norm_backward(values, gain, upstream):
    unit, inverse = normalized(values)
    scaled = upstream * gain
    inner = (
        scaled
        - jnp.mean(scaled, axis=-1, keepdims=True)
        - unit * jnp.mean(scaled * unit, axis=-1, keepdims=True)
    )
    return (inverse * inner, jnp.sum(upstream * unit, axis=0), jnp.sum(upstream, axis=0))


def silu_slope(values):
    sigma = jax.nn.sigmoid(values)
    return sigma * (1.0 + values * (1.0 - sigma))


def neighbourhood(latents):
    return padded(latents, (("edge", 0),), latents.shape[0])


def on_device(
    node_latents,
    edge_latents,
    senders,
    receivers,
    regions,
    forced,
    params,
    first_moment,
    second_moment,
    averaged,
    step,
    cotangent,
):
    latents = node_latents[0]
    edges = edge_latents[0]
    upstream = cotangent[0]
    width = latents.shape[1]
    node_rows = latents.shape[0]
    total_nodes = node_rows * lax.axis_size("edge")
    lowest = (lax.axis_index("edge") - 1) * node_rows
    send_local = jnp.mod(senders - lowest, total_nodes)
    recv_local = jnp.mod(receivers - lowest, total_nodes)
    weights = lax.all_gather(params.astype(jnp.bfloat16), "feat", axis=0, tiled=True)
    first = weights[0 : 3 * width]
    second = weights[3 * width : 4 * width]
    node_first = weights[4 * width : 6 * width]
    node_second = weights[6 * width : 7 * width]
    vectors = weights[7 * width : 7 * width + 8].astype(jnp.float32)
    table = weights[7 * width + 8 :]
    region_onehot = jax.nn.one_hot(regions, table.shape[0], dtype=jnp.bfloat16)
    near_nodes = neighbourhood(latents)
    from_send = pick_rows(near_nodes, send_local)
    from_recv = pick_rows(near_nodes, recv_local)
    pre = product(from_send, first[0:width]) + product(from_recv, first[width : 2 * width])
    pre = (
        pre
        + product(edges, first[2 * width : 3 * width])
        + vectors[0]
        + product(region_onehot, table)
    )
    hidden = jax.nn.silu(pre).astype(jnp.bfloat16)
    inner = product(hidden, second) + vectors[1]
    from_send, from_recv, pre, hidden, inner = (from_send, from_recv, pre, hidden, inner)
    messages = layer_norm(inner, vectors[2], vectors[3])
    partial_value = add_rows(messages, recv_local, 3 * node_rows)
    from_below = passed_along(partial_value[2 * node_rows :], "edge", 1)
    from_above = passed_along(partial_value[0:node_rows], "edge", -1)
    aggregate = (partial_value[node_rows : 2 * node_rows] + from_below + from_above).astype(
        jnp.bfloat16
    )
    pre_node = (
        product(latents, node_first[0:width])
        + product(aggregate, node_first[width : 2 * width])
        + vectors[4]
    )
    hidden_node = jax.nn.silu(pre_node).astype(jnp.bfloat16)
    inner_node = product(hidden_node, node_second) + vectors[5]
    update = layer_norm(inner_node, vectors[6], vectors[7])
    keep = (1 - forced).astype(jnp.float32)[:, None]
    new_latents = latents.astype(jnp.float32) + keep * update
    d_update = upstream * keep
    d_inner_node, d_gain_node, d_shift_node = norm_backward(inner_node, vectors[6], d_update)
    d_inner_node = d_inner_node.astype(jnp.bfloat16)
    g_node_second = outer_product(hidden_node, d_inner_node)
    d_bias_node_second = jnp.sum(d_inner_node.astype(jnp.float32), axis=0)
    d_pre_node = (product_transposed(d_inner_node, node_second) * silu_slope(pre_node)).astype(
        jnp.bfloat16
    )
    g_node_first = jnp.concatenate(
        [outer_product(latents, d_pre_node), outer_product(aggregate, d_pre_node)], axis=0
    )
    d_bias_node_first = jnp.sum(d_pre_node.astype(jnp.float32), axis=0)
    d_from_nodes = product_transposed(d_pre_node, node_first[0:width])
    d_aggregate = product_transposed(d_pre_node, node_first[width : 2 * width]).astype(jnp.bfloat16)
    near_back = padded(d_aggregate, (("edge", 0),), node_rows)
    d_messages = pick_rows(near_back, recv_local).astype(jnp.float32)
    d_inner, d_gain_edge, d_shift_edge = norm_backward(inner, vectors[2], d_messages)
    d_inner = d_inner.astype(jnp.bfloat16)
    g_second = outer_product(hidden, d_inner)
    d_bias_second = jnp.sum(d_inner.astype(jnp.float32), axis=0)
    d_pre = (product_transposed(d_inner, second) * silu_slope(pre)).astype(jnp.bfloat16)
    g_first = jnp.concatenate(
        [
            outer_product(from_send, d_pre),
            outer_product(from_recv, d_pre),
            outer_product(edges, d_pre),
        ],
        axis=0,
    )
    d_bias_first = jnp.sum(d_pre.astype(jnp.float32), axis=0)
    g_table = outer_product(region_onehot, d_pre)
    d_send = product_transposed(d_pre, first[0:width])
    d_recv = product_transposed(d_pre, first[width : 2 * width])
    grad_edges = product_transposed(d_pre, first[2 * width : 3 * width]).astype(jnp.bfloat16)
    node_partial = add_rows(d_send, send_local, 3 * node_rows) + add_rows(
        d_recv, recv_local, 3 * node_rows
    )
    grads_below = passed_along(
        node_partial[2 * node_rows :].astype(jnp.bfloat16), "edge", 1
    ).astype(jnp.float32)
    grads_above = passed_along(node_partial[0:node_rows].astype(jnp.bfloat16), "edge", -1).astype(
        jnp.float32
    )
    d_nodes = node_partial[node_rows : 2 * node_rows] + grads_below + grads_above
    grad_latents = upstream + d_from_nodes + d_nodes
    vector_rows = jnp.stack(
        [
            d_bias_first,
            d_bias_second,
            d_gain_edge,
            d_shift_edge,
            d_bias_node_first,
            d_bias_node_second,
            d_gain_node,
            d_shift_node,
        ],
        axis=0,
    )
    local_grad = jnp.concatenate(
        [g_first, g_second, g_node_first, g_node_second, vector_rows, g_table], axis=0
    )
    share = params.shape[0]
    summed = lax.psum(local_grad, ("edge", "feat"))
    owned = lax.dynamic_slice_in_dim(summed, lax.axis_index("feat") * share, share, 0)
    rows_here = lax.axis_index("feat") * share + lax.broadcasted_iota(jnp.int32, (8, share), 1)
    wanted = 7 * width + lax.broadcasted_iota(jnp.int32, (8, share), 0)
    select = (rows_here == wanted).astype(jnp.float32)
    vector_piece = jnp.dot(
        select, owned, precision=lax.Precision.HIGHEST, preferred_element_type=jnp.float32
    )
    squares, vector_total = lax.psum((jnp.sum(owned * owned), vector_piece), "feat")
    grad_norm = jnp.sqrt(squares)
    factor = jnp.minimum(1.0, MAX_NORM / (grad_norm + 1e-06))
    clipped = owned * factor
    vector_grads = vector_total * factor
    new_first = BETA_ONE * first_moment + (1.0 - BETA_ONE) * clipped
    new_second = BETA_TWO * second_moment + (1.0 - BETA_TWO) * clipped * clipped
    count_steps = step[0].astype(jnp.float32)
    first_hat = new_first / (1.0 - jnp.power(BETA_ONE, count_steps))
    second_hat = new_second / (1.0 - jnp.power(BETA_TWO, count_steps))
    new_params = params - RATE * (
        first_hat / (jnp.sqrt(second_hat) + ADAM_EPS) + WEIGHT_DECAY * params
    )
    decay_now = jnp.minimum(AVERAGE_DECAY, (1.0 + count_steps) / (10.0 + count_steps))
    new_average = decay_now * averaged + (1.0 - decay_now) * new_params
    return (
        new_latents[None],
        grad_latents[None],
        grad_edges[None],
        new_first,
        new_second,
        new_params,
        new_average,
        grad_norm.reshape(1),
        vector_grads,
    )


def solution(mesh):
    placed = (
        P("feat", "edge", None),
        P("feat", "edge", None),
        P("edge"),
        P("edge"),
        P("edge"),
        P("edge"),
        P("feat", None),
        P("feat", None),
        P("feat", None),
        P("feat", None),
        P(),
        P("feat", "edge", None),
    )
    return jax.shard_map(
        on_device,
        mesh=mesh,
        in_specs=placed,
        out_specs=(
            P("feat", "edge", None),
            P("feat", "edge", None),
            P("feat", "edge", None),
            P("feat", None),
            P("feat", None),
            P("feat", None),
            P("feat", None),
            P(),
            P(),
        ),
        check_vma=False,
    )
```

profile of v0, /device:TPU:0, one launch (start us, length us, event | category | flops | bytes accessed | tf_op | source)
XLA Modules:
  0.0 374.1 jit_solution(12631992785596046417)
XLA Ops:
  7.2 1.2 copy.42
  9.0 2.9 collective-permute-start.1
  12.7 1.0 convert_element_type.71
  13.8 22.2 %all_gather.3 = bf16[1824,256]{1,0:T(8,128)(2,1)S(1)} all-gather(bf16[456,256]{1,0:T(8,128)(2,1)S(1)} %convert_element_type.71), channel_id=1, replica_groups=mesh['edge'=8,'feat'=4] {'feat'}, dimensions={0}, use_global_device_ids=true | all-gather | bytes 1167360 | tf_op jit(solution)/shard_map/all_gather | solution.py:117
  36.0 0.9 copy-done.10
  37.0 0.9 pad_maximum_fusion
  37.9 1.4 copy.43
  39.3 17.0 %gather_fusion = bf16[4096,256]{1,0:T(8,128)(2,1)} fusion(bf16[1536,256]{1,0:T(8,128)(2,1)S(1)} %copy.43, s32[4096]{0:T(1024)S(1)} %fusion.66), kind=kCustom, calls=%fused_computation.clone | custom fusion | bytes 4210688 | tf_op jit(solution)/shard_map/jit(_take)/gather | solution.py:55
  56.4 16.9 %gather_fusion.1 = bf16[4096,256]{1,0:T(8,128)(2,1)} fusion(bf16[1536,256]{1,0:T(8,128)(2,1)S(1)} %copy.43, s32[4096]{0:T(1024)S(1)} %fusion.67), kind=kCustom, calls=%fused_computation.1.clone | custom fusion | bytes 4210688 | tf_op jit(solution)/shard_map/jit(_take)/gather | solution.py:55
  73.3 4.0 %fusion.20 = f32[4096,256]{1,0:T(8,128)S(1)} fusion(bf16[4096,256]{1,0:T(8,128)(2,1)} %gather_fusion, pred[4096]{0:T(1024)(128)(4,1)S(1)} %get-tuple-element.86, bf16[1824,256]{1,0:T(8,128)(2,1)} %copy-done.10), kind=kOutput, calls=%fused_computation.49 | convolution fusion | flops 537919488 | bytes 6426624 | tf_op jit(solution)/shard_map/dot_general | solution.py:39
  77.3 1.7 convolution_add_fusion.3
  79.0 1.7 fusion.3
  80.7 4.0 %multiply_convert_fusion = (bf16[4096,256]{1,0:T(8,128)(2,1)S(1)}, f32[4096,256]{1,0:T(8,128)}) fusion(f32[4096,256]{1,0:T(8,128)S(1)} %fusion.3, bf16[1824,256]{1,0:T(8,128)(2,1)} %copy-done.10, s32[4096]{0:T(1024)S(1)} %copy-done.23), kind=kOutput, calls=%fused_computation.30 | convolution fusion | flops 56721408 | bytes 10514432 | tf_op jit(solution)/shard_map/dot_general | solution.py:39
  84.7 1.8 fusion.82
  87.0 1.5 copy-done.1
  88.5 2.7 multiply_add_fusion
  91.2 5.6 %copy.45 = f32[4096,256]{1,0:T(8,128)} copy(f32[4096,256]{0,1:T(8,128)} %multiply_add_fusion) | data formatting | bytes 8388608 | tf_op jit(solution)/shard_map/add | solution.py:71
  96.8 24.1 %scatter_custom_fusion = f32[1536,256]{1,0:T(8,128)} fusion(s32[4096]{0:T(1024)S(1)} %get-tuple-element.58, f32[4096,256]{1,0:T(8,128)} %copy.45, f32[]{:T(128)} %constant.42.clone.1), kind=kCustom, calls=%fused_computation.57 | custom fusion | flops 1048576 | bytes 1573376 | tf_op jit(solution)/shard_map/scatter-add | solution.py:59
  120.9 2.2 fusion.79
  123.2 2.6 collective-permute-start.3
  126.4 1.2 copy.46
  127.7 1.1 fusion.41
  128.8 8.7 %collective-permute-done.2 = f32[512,256]{1,0:T(8,128)S(1)} collective-permute-done((f32[512,256]{1,0:T(8,128)}, f32[512,256]{1,0:T(8,128)S(1)}, u32[]{:S(2)}, u32[]{:S(2)}) %collective-permute-start.2) | collective-permute-done | bytes 524320 | tf_op jit(solution)/shard_map/ppermute | solution.py:35
  137.5 0.8 copy-done.21
  138.3 1.4 fusion.32
  139.8 1.3 multiply_convert_fusion.2
  141.1 1.2 fusion.83
  142.7 1.1 convert_reduce_fusion.3
  143.8 1.0 fusion.86
  144.8 1.2 convert_reduce_fusion.4
  146.1 1.3 convolution_convert_fusion.1
  147.4 2.6 collective-permute-start.5
  150.0 1.0 fusion.85
  151.0 1.0 convolution_bitcast_fusion
  152.0 4.5 %collective-permute-done.4 = bf16[512,256]{1,0:T(8,128)(2,1)S(1)} collective-permute-done((bf16[512,256]{1,0:T(8,128)(2,1)S(1)}, bf16[512,256]{1,0:T(8,128)(2,1)S(1)}, u32[]{:S(2)}, u32[]{:S(2)}) %collective-permute-start.4) | collective-permute-done | bytes 262176 | tf_op jit(solution)/shard_map/ppermute | solution.py:23
  156.6 16.9 %gather_fusion.2 = bf16[4096,256]{1,0:T(8,128)(2,1)} fusion(bf16[1536,256]{1,0:T(8,128)(2,1)S(1)} %pad_maximum_fusion.1, s32[4096]{0:T(1024)S(1)} %fusion.67), kind=kCustom, calls=%fused_computation.2.clone | custom fusion | bytes 4210688 | tf_op jit(solution)/shard_map/jit(_take)/gather | solution.py:55
  173.5 4.1 %copy.48 = bf16[4096,256]{0,1:T(8,128)(2,1)} copy(bf16[4096,256]{1,0:T(8,128)(2,1)} %gather_fusion.2) | data formatting | bytes 4194304 | tf_op jit(solution)/shard_map/jit(_take)/gather | solution.py:55
  177.6 5.3 %fusion.10 = (f32[256]{0:T(256)S(1)}, f32[4096]{0:T(1024)S(1)}, f32[4096]{0:T(1024)S(1)}, f32[256]{0:T(256)S(1)}) fusion(f32[4096,256]{0,1:T(8,128)} %copy-done.1, f32[4096]{0:T(1024)S(1)} %add_rsqrt_fusion, f32[4096]{0:T(1024)S(1)} %broadcast_multiply_fusion.2, bf16[4096,256]{0,1:T(8,128)(2,1)} %copy.48, pred[4096]{0:T(1024)(128)(4,1)S(1)} %get-tuple-element.57, ...), kind=kLoop, calls=%fused_computation.25 | loop fusion | flops 11525632 | bytes 6364160 | tf_op jit(solution)/shard_map/reduce_sum | solution.py:82
  183.0 2.3 convert_reduce_fusion.1
  185.3 1.5 fusion.84
  186.8 0.8 copy-done.25
  187.6 3.0 convert_reduce_fusion.2
  190.6 2.1 fusion.19
  192.9 2.1 fusion.21
  195.1 1.7 fusion.16
  197.1 3.6 fusion.53
  200.8 3.8 %fusion.56 = f32[4096,256]{1,0:T(8,128)} fusion(bf16[4096,256]{1,0:T(8,128)(2,1)S(1)} %get-tuple-element.83, bf16[1824,256]{1,0:T(8,128)(2,1)} %copy-done.10), kind=kOutput, calls=%fused_computation.106 | convolution fusion | flops 536870912 | bytes 6422528 | tf_op jit(solution)/shard_map/dot_general | solution.py:49
  204.6 10.1 %concatenate.11 = f32[1824,256]{1,0:T(8,128)} concatenate(f32[256,256]{1,0:T(8,128)} %fusion.19, f32[256,256]{1,0:T(8,128)} %fusion.21, f32[256,256]{1,0:T(8,128)} %fusion.16, f32[256,256]{1,0:T(8,128)} %fusion.84, f32[256,256]{1,0:T(8,128)S(1)} %copy-done.20, f32[256,256]{1,0:T(8,128)S(1)} %copy-done.19, f32[256,256]{1,0:T(8,128)S(1)} %copy-done.18, f32[1,256]{1,0:T(1,128)S(1)} %bitcast.104, ...), dimensions={0} | concatenate | bytes 3735552 | tf_op jit(solution)/shard_map/concatenate | solution.py:213
  214.7 24.0 %scatter_custom_fusion.2 = f32[1536,256]{1,0:T(8,128)} fusion(s32[4096]{0:T(1024)S(1)} %get-tuple-element.58, f32[4096,256]{1,0:T(8,128)} %fusion.53, f32[]{:T(128)} %constant.42.clone.1), kind=kCustom, calls=%fused_computation.53 | custom fusion | flops 1048576 | bytes 1573376 | tf_op jit(solution)/shard_map/scatter-add | solution.py:59
  238.8 3.1 copy.50
  241.9 24.0 %scatter_custom_fusion.1 = f32[1536,256]{1,0:T(8,128)} fusion(s32[4096]{0:T(1024)S(1)} %get-tuple-element.87, f32[4096,256]{1,0:T(8,128)} %fusion.56, f32[]{:T(128)} %constant.42.clone.1), kind=kCustom, calls=%fused_computation.55 | custom fusion | flops 1048576 | bytes 1573376 | tf_op jit(solution)/shard_map/scatter-add | solution.py:59
  265.9 3.1 copy.49
  269.0 3.4 fusion.78
  272.4 0.8 fusion.80
  273.2 2.6 collective-permute-start.7
  277.1 1.0 copy.51
  278.1 3.7 fusion.5
  282.0 1.4 fusion.30
  283.5 61.5 %all-reduce.3.cloned.1.call-done = f32[1824,256]{1,0:T(8,128)} async-done(((f32[1824,256]{1,0:T(8,128)}), f32[1824,256]{1,0:T(8,128)}) %all-reduce.3.cloned.1.call-update) | async-done | bytes 1867792 | tf_op jit(solution)/shard_map/psum | solution.py:217
  344.9 1.7 multiply_reduce_fusion.4
  346.7 1.9 fusion.38
  348.6 1.0 copy.52
  349.6 12.4 %all-reduce = (f32[]{:T(128)}, f32[8,256]{1,0:T(8,128)S(1)}) all-reduce(f32[]{:T(128)} %multiply_reduce_fusion.4, f32[8,256]{1,0:T(8,128)} %fusion.38), channel_id=1, replica_groups=mesh['edge'=8,'feat'=4] {'feat'}, use_global_device_ids=true, to_apply=%region_21.23 | all-reduce | flops 2049 | bytes 16392 | tf_op jit(solution)/shard_map/psum | solution.py:225
  363.3 2.8 multiply_add_fusion.1
  (82 shorter events, 5.0 us)
Async XLA Ops:
  7.2 71.8 %copy-start = (bf16[1,4096,256]{2,1,0:T(8,128)(2,1)S(1)}, bf16[1,4096,256]{2,1,0:T(8,128)(2,1)}, u32[]{:S(2)}) copy-start(bf16[1,4096,256]{2,1,0:T(8,128)(2,1)} %param.15) | copy-start | bytes 6291460
  7.2 337.8 %all-reduce.3.cloned.1.call-start = ((), (), s32[]{:S(2)}) async-start(), calls=%async_computation | async-start | bytes 3735552 | tf_op jit(solution)/shard_map/psum | solution.py:217
  8.5 28.5 %copy-start.14 = (bf16[1,512,256]{1,2,0:T(8,128)(2,1)}, bf16[1,512,256]{1,2,0:T(8,128)(2,1)S(1)}, u32[]{:S(2)}) copy-start(bf16[1,512,256]{1,2,0:T(8,128)(2,1)S(1)} %copy.42) | copy-start | bytes 786436
  8.5 28.5 %collective-permute-start = (bf16[512,256]{0,1:T(8,128)(2,1)S(1)}, bf16[512,256]{0,1:T(8,128)(2,1)S(1)}, u32[]{:S(2)}, u32[]{:S(2)}) collective-permute-start(bf16[512,256]{0,1:T(8,128)(2,1)S(1)} %bitcast.84), channel_id=1, source_target_pairs={{0,4},{4,8},{8,12},{12,16},{16,20},{20,24},{24,28},{28,0},{1,5},{5... | collective-permute-start | bytes 786440 | tf_op jit(solution)/shard_map/ppermute | solution.py:23
  9.0 28.0 %collective-permute-start.1 = (bf16[512,256]{0,1:T(8,128)(2,1)S(1)}, bf16[512,256]{0,1:T(8,128)(2,1)S(1)}, u32[]{:S(2)}, u32[]{:S(2)}) collective-permute-start(bf16[512,256]{0,1:T(8,128)(2,1)S(1)} %bitcast.85), channel_id=1, source_target_pairs={{4,0},{8,4},{12,8},{16,12},{20,16},{24,20},{28,24},{0,28},{5,1},{9... | collective-permute-start | bytes 786440 | tf_op jit(solution)/shard_map/ppermute | solution.py:25
  36.0 0.9 copy-start.10
  73.3 4.0 %copy-start.8 = (bf16[4096,256]{1,0:T(8,128)(2,1)S(1)}, bf16[4096,256]{1,0:T(8,128)(2,1)}, u32[]{:S(2)}) copy-start(bf16[4096,256]{1,0:T(8,128)(2,1)} %gather_fusion.1) | copy-start | bytes 6291460
  79.0 1.7 copy-start.23
  84.7 1.8 copy-start.6
  86.5 2.0 copy-start.1
  96.8 30.8 %copy-start.24 = (s32[512]{0:T(512)S(1)}, s32[512]{0:T(512)}, u32[]{:S(2)}) copy-start(s32[512]{0:T(512)} %param.19) | copy-start | bytes 6148
  96.8 30.8 %copy-start.13 = (bf16[1,512,256]{2,1,0:T(8,128)(2,1)S(1)}, bf16[1,512,256]{2,1,0:T(8,128)(2,1)}, u32[]{:S(2)}) copy-start(bf16[1,512,256]{2,1,0:T(8,128)(2,1)} %param.14) | copy-start | bytes 786436
  123.2 14.4 %collective-permute-start.2 = (f32[512,256]{1,0:T(8,128)}, f32[512,256]{1,0:T(8,128)S(1)}, u32[]{:S(2)}, u32[]{:S(2)}) collective-permute-start(f32[512,256]{1,0:T(8,128)} %get-tuple-element.61), channel_id=1, source_target_pairs={{0,4},{4,8},{8,12},{12,16},{16,20},{20,24},{24,28},{28,0},{1,5},{5... | collective-permute-start | bytes 1572872 | tf_op jit(solution)/shard_map/ppermute | solution.py:35
  123.2 15.2 %collective-permute-start.3 = (f32[512,256]{1,0:T(8,128)}, f32[512,256]{1,0:T(8,128)}, u32[]{:S(2)}, u32[]{:S(2)}) collective-permute-start(f32[512,256]{1,0:T(8,128)} %get-tuple-element.62), channel_id=1, source_target_pairs={{0,28},{4,0},{8,4},{12,8},{16,12},{20,16},{24,20},{28,24},{1,29},{... | collective-permute-start | bytes 1572872 | tf_op jit(solution)/shard_map/ppermute | solution.py:35
  137.5 0.8 copy-start.21
  139.8 2.9 copy-start.15
  146.0 10.5 %copy-start.11 = (bf16[512,256]{1,0:T(8,128)(2,1)}, bf16[512,256]{1,0:T(8,128)(2,1)S(1)}, u32[]{:S(2)}) copy-start(bf16[512,256]{1,0:T(8,128)(2,1)S(1)} %get-tuple-element.85) | copy-start | bytes 786436
  147.3 9.2 %collective-permute-start.4 = (bf16[512,256]{1,0:T(8,128)(2,1)S(1)}, bf16[512,256]{1,0:T(8,128)(2,1)S(1)}, u32[]{:S(2)}, u32[]{:S(2)}) collective-permute-start(bf16[512,256]{1,0:T(8,128)(2,1)S(1)} %convolution_convert_fusion.1), channel_id=1, source_target_pairs={{0,4},{4,8},{8,12},{12,16},{16,20},{20,24},{24,28},{28,0},{1,5},{5... | collective-permute-start | bytes 786440 | tf_op jit(solution)/shard_map/ppermute | solution.py:23
  147.4 9.1 %collective-permute-start.5 = (bf16[512,256]{1,0:T(8,128)(2,1)S(1)}, bf16[512,256]{1,0:T(8,128)(2,1)S(1)}, u32[]{:S(2)}, u32[]{:S(2)}) collective-permute-start(bf16[512,256]{1,0:T(8,128)(2,1)S(1)} %convolution_convert_fusion.1), channel_id=1, source_target_pairs={{4,0},{8,4},{12,8},{16,12},{20,16},{24,20},{28,24},{0,28},{5,1},{9... | collective-permute-start | bytes 786440 | tf_op jit(solution)/shard_map/ppermute | solution.py:25
  177.6 5.4 %copy-start.2 = (f32[4096,256]{0,1:T(8,128)S(1)}, f32[4096,256]{0,1:T(8,128)}, u32[]{:S(2)}) copy-start(f32[4096,256]{0,1:T(8,128)} %copy-done.1) | copy-start | bytes 12582916
  177.6 5.4 %copy-start.4 = (bf16[4096,256]{0,1:T(8,128)(2,1)S(1)}, bf16[4096,256]{0,1:T(8,128)(2,1)}, u32[]{:S(2)}) copy-start(bf16[4096,256]{0,1:T(8,128)(2,1)} %copy.48) | copy-start | bytes 6291460
  183.0 2.3 copy-start.7
  185.3 2.3 copy-start.25
  187.6 3.0 copy-start.5
  190.6 10.2 %copy-start.3 = (bf16[4096,256]{1,0:T(8,128)(2,1)}, bf16[4096,256]{1,0:T(8,128)(2,1)S(1)}, u32[]{:S(2)}) copy-start(bf16[4096,256]{1,0:T(8,128)(2,1)S(1)} %get-tuple-element.83) | copy-start | bytes 6291460
  190.6 2.3 copy-start.9
  200.8 3.8 %copy-start.18 = (f32[256,256]{1,0:T(8,128)S(1)}, f32[256,256]{1,0:T(8,128)}, u32[]{:S(2)}) copy-start(f32[256,256]{1,0:T(8,128)} %fusion.86) | copy-start | bytes 786436
  200.8 3.8 %copy-start.19 = (f32[256,256]{1,0:T(8,128)S(1)}, f32[256,256]{1,0:T(8,128)}, u32[]{:S(2)}) copy-start(f32[256,256]{1,0:T(8,128)} %fusion.85) | copy-start | bytes 786436
  200.8 3.8 %copy-start.20 = (f32[256,256]{1,0:T(8,128)S(1)}, f32[256,256]{1,0:T(8,128)}, u32[]{:S(2)}) copy-start(f32[256,256]{1,0:T(8,128)} %convolution_bitcast_fusion) | copy-start | bytes 786436
  269.0 8.2 %copy-start.16 = (f32[1,512,256]{1,2,0:T(8,128)S(1)}, f32[1,512,256]{1,2,0:T(8,128)}, u32[]{:S(2)}) copy-start(f32[1,512,256]{1,2,0:T(8,128)} %get-tuple-element.65) | copy-start | bytes 1572868
  273.2 8.8 %collective-permute-start.6 = (bf16[512,256]{0,1:T(8,128)(2,1)}, bf16[512,256]{0,1:T(8,128)(2,1)S(1)}, u32[]{:S(2)}, u32[]{:S(2)}) collective-permute-start(bf16[512,256]{0,1:T(8,128)(2,1)} %get-tuple-element.63), channel_id=1, source_target_pairs={{0,4},{4,8},{8,12},{12,16},{16,20},{20,24},{24,28},{28,0},{1,5},{5... | collective-permute-start | bytes 786440 | tf_op jit(solution)/shard_map/ppermute | solution.py:35
  273.2 8.8 %collective-permute-start.7 = (bf16[512,256]{0,1:T(8,128)(2,1)}, bf16[512,256]{0,1:T(8,128)(2,1)}, u32[]{:S(2)}, u32[]{:S(2)}) collective-permute-start(bf16[512,256]{0,1:T(8,128)(2,1)} %get-tuple-element.64), channel_id=1, source_target_pairs={{0,28},{4,0},{8,4},{12,8},{16,12},{20,16},{24,20},{28,24},{1,29},{... | collective-permute-start | bytes 786440 | tf_op jit(solution)/shard_map/ppermute | solution.py:35
  278.1 3.9 %copy-start.12 = (bf16[512,256]{1,0:T(8,128)(2,1)S(1)}, bf16[512,256]{1,0:T(8,128)(2,1)}, u32[]{:S(2)}) copy-start(bf16[512,256]{1,0:T(8,128)(2,1)} %copy-done.11) | copy-start | bytes 786436
  283.5 79.8 %copy-start.17 = (f32[456,256]{1,0:T(8,128)S(1)}, f32[456,256]{1,0:T(8,128)}, u32[]{:S(2)}) copy-start(f32[456,256]{1,0:T(8,128)} %param.20) | copy-start | bytes 1400836
  283.5 79.8 %copy-start.22 = (f32[456,256]{1,0:T(8,128)S(1)}, f32[456,256]{1,0:T(8,128)}, u32[]{:S(2)}) copy-start(f32[456,256]{1,0:T(8,128)} %param.23) | copy-start | bytes 1400836
Sparse Core Ops, SparseCore 0:
  214.8 130.0 all-reduce.2
where the time goes:
time: 375 us; the launch traced here: 374 us
  other arithmetic  98.5 us (26%)
  local copies, waits for them, and re-layouts  90 us (24%)
  waiting for transfers between devices  74.9 us (20%)
  matrix products  47.4 us (13%)
  blocking collectives  34.6 us (9%)
  between operations  17.2 us (5%)
  starting transfers between devices  11.5 us (3%)
    scatter-add x3, other arithmetic, add_rows(): return jax.ops.segment_sum(values, indices, num_segments=rows)  72.2 us
    psum x1, waiting for transfers between devices, on_device(): summed = lax.psum(local_grad, ('edge', 'feat'))  61.5 us
    gather x4, local copies, waits for them, and re-layouts, pick_rows(): return jnp.take(table, indices, axis=0)  55 us
    all_gather x1, blocking collectives, on_device(): lax.all_gather(params.astype(jnp.bfloat16), 'feat', axis=0, tiled=True)  22.2 us
    dot_general x7, matrix products, product_transposed(): lax.dot_general(left, right, (((1,), (1,)), ((), ())), preferred_element_...  18 us
    dot_general x8, matrix products, product(): return jnp.dot(left, right, preferred_element_type=jnp.float32)  16.7 us
    psum x1, blocking collectives, on_device(): lax.psum((jnp.sum(owned * owned), vector_piece), 'feat')  12.4 us
    dot_general x8, matrix products, outer_product(): lax.dot_general(left, right, (((0,), (0,)), ((), ())), preferred_element_...  10.7 us
  transfers between devices with their start and end apart: 9, of which 4 were waited for; matrix products, arithmetic and copies ran while one was open for 19% of the time, Pallas kernels for 0%

commit v1 on v0

--- a/solution.py
+++ b/solution.py
@@ -214,7 +214,8 @@
         [g_first, g_second, g_node_first, g_node_second, vector_rows, g_table], axis=0
     )
     share = params.shape[0]
-    summed = lax.psum(local_grad, ("edge", "feat"))
+    half = lax.psum(local_grad, "feat")
+    summed = lax.psum(half, "edge")
     owned = lax.dynamic_slice_in_dim(summed, lax.axis_index("feat") * share, share, 0)
     rows_here = lax.axis_index("feat") * share + lax.broadcasted_iota(jnp.int32, (8, share), 1)
     wanted = 7 * width + lax.broadcasted_iota(jnp.int32, (8, share), 0)

time: 375 us -> 380 us (1.013)
    ppermute x4, waiting for transfers between devices: 8.93 us -> 13.6 us  [passed_along(): return lax.ppermute(value, axis, pairs)]
    psum x1 -> x2, waiting for transfers between devices: 61.5 us -> 59 us  [the longest x1 46 us: on_device(): summed = lax.psum(half, 'edge')]
  transfers between devices with their start and end apart: 9 -> 10, of which waited for: 4 -> 6; matrix products, arithmetic and copies ran while one was open for 19% -> 21% of each run, Pallas kernels for 0% -> 0%
where the time goes in v1:
time: 380 us; the launch traced here: 379 us
  other arithmetic  98.4 us (26%)
  local copies, waits for them, and re-layouts  90.7 us (24%)
  waiting for transfers between devices  77.1 us (20%)
  matrix products  48.5 us (13%)
  blocking collectives  34.9 us (9%)
  between operations  17.2 us (5%)
  starting transfers between devices  11.7 us (3%)
    scatter-add x3, other arithmetic, add_rows(): return jax.ops.segment_sum(values, indices, num_segments=rows)  72.2 us
    gather x4, local copies, waits for them, and re-layouts, pick_rows(): return jnp.take(table, indices, axis=0)  55 us
    psum x1, waiting for transfers between devices, on_device(): summed = lax.psum(half, 'edge')  46 us
    all_gather x1, blocking collectives, on_device(): lax.all_gather(params.astype(jnp.bfloat16), 'feat', axis=0, tiled=True)  22.2 us
    dot_general x7, matrix products, product_transposed(): lax.dot_general(left, right, (((1,), (1,)), ((), ())), preferred_element_...  19.1 us
    dot_general x8, matrix products, product(): return jnp.dot(left, right, preferred_element_type=jnp.float32)  16.7 us
    ppermute x4, waiting for transfers between devices, passed_along(): return lax.ppermute(value, axis, pairs)  13.6 us
    psum x1, waiting for transfers between devices, on_device(): half = lax.psum(local_grad, 'feat')  12.9 us
  transfers between devices with their start and end apart: 10, of which 6 were waited for; matrix products, arithmetic and copies ran while one was open for 21% of the time, Pallas kernels for 0%

profile of v1, /device:TPU:0, one launch (start us, length us, event | category | flops | bytes accessed | tf_op | source)
XLA Modules:
  0.0 378.6 jit_solution(9382470679849543556)
XLA Ops:
  7.2 1.2 copy.42
  9.0 2.9 collective-permute-start.1
  12.7 1.0 convert_element_type.71
  13.8 22.2 %all_gather.3 = bf16[1824,256]{1,0:T(8,128)(2,1)S(1)} all-gather(bf16[456,256]{1,0:T(8,128)(2,1)S(1)} %convert_element_type.71), channel_id=1, replica_groups=mesh['edge'=8,'feat'=4] {'feat'}, dimensions={0}, use_global_device_ids=true | all-gather | bytes 1167360 | tf_op jit(solution)/shard_map/all_gather | solution.py:117
  36.0 0.9 copy-done.10
  37.0 0.9 pad_maximum_fusion
  37.9 1.4 copy.43
  39.3 17.0 %gather_fusion = bf16[4096,256]{1,0:T(8,128)(2,1)} fusion(bf16[1536,256]{1,0:T(8,128)(2,1)S(1)} %copy.43, s32[4096]{0:T(1024)S(1)} %fusion.66), kind=kCustom, calls=%fused_computation.clone | custom fusion | bytes 4210688 | tf_op jit(solution)/shard_map/jit(_take)/gather | solution.py:55
  56.4 16.9 %gather_fusion.1 = bf16[4096,256]{1,0:T(8,128)(2,1)} fusion(bf16[1536,256]{1,0:T(8,128)(2,1)S(1)} %copy.43, s32[4096]{0:T(1024)S(1)} %fusion.67), kind=kCustom, calls=%fused_computation.1.clone | custom fusion | bytes 4210688 | tf_op jit(solution)/shard_map/jit(_take)/gather | solution.py:55
  73.3 4.0 %fusion.20 = f32[4096,256]{1,0:T(8,128)S(1)} fusion(bf16[4096,256]{1,0:T(8,128)(2,1)} %gather_fusion, pred[4096]{0:T(1024)(128)(4,1)S(1)} %get-tuple-element.86, bf16[1824,256]{1,0:T(8,128)(2,1)} %copy-done.10), kind=kOutput, calls=%fused_computation.49 | convolution fusion | flops 537919488 | bytes 6426624 | tf_op jit(solution)/shard_map/dot_general | solution.py:39
  77.3 1.7 convolution_add_fusion.3
  79.0 1.7 fusion.3
  80.7 4.0 %multiply_convert_fusion = (bf16[4096,256]{1,0:T(8,128)(2,1)S(1)}, f32[4096,256]{1,0:T(8,128)}) fusion(f32[4096,256]{1,0:T(8,128)S(1)} %fusion.3, bf16[1824,256]{1,0:T(8,128)(2,1)} %copy-done.10, s32[4096]{0:T(1024)S(1)} %copy-done.23), kind=kOutput, calls=%fused_computation.30 | convolution fusion | flops 56721408 | bytes 10514432 | tf_op jit(solution)/shard_map/dot_general | solution.py:39
  84.7 1.8 fusion.82
  87.0 1.5 copy-done.1
  88.5 2.7 multiply_add_fusion
  91.2 5.6 %copy.45 = f32[4096,256]{1,0:T(8,128)} copy(f32[4096,256]{0,1:T(8,128)} %multiply_add_fusion) | data formatting | bytes 8388608 | tf_op jit(solution)/shard_map/add | solution.py:71
  96.8 24.1 %scatter_custom_fusion = f32[1536,256]{1,0:T(8,128)} fusion(s32[4096]{0:T(1024)S(1)} %get-tuple-element.58, f32[4096,256]{1,0:T(8,128)} %copy.45, f32[]{:T(128)} %constant.42.clone.1), kind=kCustom, calls=%fused_computation.57 | custom fusion | flops 1048576 | bytes 1573376 | tf_op jit(solution)/shard_map/scatter-add | solution.py:59
  120.9 2.2 fusion.79
  123.2 2.6 collective-permute-start.3
  125.8 1.2 copy.46
  127.1 1.1 fusion.41
  128.2 9.3 %collective-permute-done.2 = f32[512,256]{1,0:T(8,128)S(1)} collective-permute-done((f32[512,256]{1,0:T(8,128)}, f32[512,256]{1,0:T(8,128)S(1)}, u32[]{:S(2)}, u32[]{:S(2)}) %collective-permute-start.2) | collective-permute-done | bytes 524320 | tf_op jit(solution)/shard_map/ppermute | solution.py:35
  138.4 1.4 fusion.32
  139.8 1.3 multiply_convert_fusion.2
  141.1 1.2 fusion.83
  142.7 1.1 convert_reduce_fusion.3
  143.8 1.0 fusion.86
  144.8 1.2 convert_reduce_fusion.4
  146.1 1.3 convolution_convert_fusion.1
  147.4 2.6 collective-permute-start.5
  150.0 1.0 fusion.85
  151.0 1.0 convolution_bitcast_fusion
  152.0 4.5 %collective-permute-done.4 = bf16[512,256]{1,0:T(8,128)(2,1)S(1)} collective-permute-done((bf16[512,256]{1,0:T(8,128)(2,1)S(1)}, bf16[512,256]{1,0:T(8,128)(2,1)S(1)}, u32[]{:S(2)}, u32[]{:S(2)}) %collective-permute-start.4) | collective-permute-done | bytes 262176 | tf_op jit(solution)/shard_map/ppermute | solution.py:23
  156.6 16.9 %gather_fusion.2 = bf16[4096,256]{1,0:T(8,128)(2,1)} fusion(bf16[1536,256]{1,0:T(8,128)(2,1)S(1)} %pad_maximum_fusion.1, s32[4096]{0:T(1024)S(1)} %fusion.67), kind=kCustom, calls=%fused_computation.2.clone | custom fusion | bytes 4210688 | tf_op jit(solution)/shard_map/jit(_take)/gather | solution.py:55
  173.5 4.1 %copy.48 = bf16[4096,256]{0,1:T(8,128)(2,1)} copy(bf16[4096,256]{1,0:T(8,128)(2,1)} %gather_fusion.2) | data formatting | bytes 4194304 | tf_op jit(solution)/shard_map/jit(_take)/gather | solution.py:55
  177.6 5.3 %fusion.10 = (f32[256]{0:T(256)S(1)}, f32[4096]{0:T(1024)S(1)}, f32[4096]{0:T(1024)S(1)}, f32[256]{0:T(256)S(1)}) fusion(f32[4096,256]{0,1:T(8,128)} %copy-done.1, f32[4096]{0:T(1024)S(1)} %add_rsqrt_fusion, f32[4096]{0:T(1024)S(1)} %broadcast_multiply_fusion.2, bf16[4096,256]{0,1:T(8,128)(2,1)} %copy.48, pred[4096]{0:T(1024)(128)(4,1)S(1)} %get-tuple-element.57, ...), kind=kLoop, calls=%fused_computation.25 | loop fusion | flops 11525632 | bytes 6364160 | tf_op jit(solution)/shard_map/reduce_sum | solution.py:82
  183.0 2.3 convert_reduce_fusion.1
  185.3 1.5 fusion.84
  187.6 3.0 convert_reduce_fusion.2
  190.6 2.1 fusion.19
  192.9 2.1 fusion.21
  195.1 1.7 fusion.16
  197.9 10.1 %concatenate.11 = f32[1824,256]{1,0:T(8,128)} concatenate(f32[256,256]{1,0:T(8,128)} %fusion.19, f32[256,256]{1,0:T(8,128)} %fusion.21, f32[256,256]{1,0:T(8,128)} %fusion.16, f32[256,256]{1,0:T(8,128)} %fusion.84, f32[256,256]{1,0:T(8,128)S(1)} %copy-done.20, f32[256,256]{1,0:T(8,128)S(1)} %copy-done.19, f32[256,256]{1,0:T(8,128)S(1)} %copy-done.18, f32[1,256]{1,0:T(1,128)S(1)} %bitcast.104, ...), dimensions={0} | concatenate | bytes 3735552 | tf_op jit(solution)/shard_map/concatenate | solution.py:213
  208.8 4.3 %fusion.53 = f32[4096,256]{1,0:T(8,128)} fusion(bf16[4096,256]{1,0:T(8,128)(2,1)} %copy-done.3, bf16[1824,256]{1,0:T(8,128)(2,1)} %copy-done.10), kind=kOutput, calls=%fused_computation.103 | convolution fusion | flops 536870912 | bytes 6422528 | tf_op jit(solution)/shard_map/dot_general | solution.py:49
  213.1 24.0 %scatter_custom_fusion.2 = f32[1536,256]{1,0:T(8,128)} fusion(s32[4096]{0:T(1024)S(1)} %get-tuple-element.58, f32[4096,256]{1,0:T(8,128)} %fusion.53, f32[]{:T(128)} %constant.42.clone.1), kind=kCustom, calls=%fused_computation.53 | custom fusion | flops 1048576 | bytes 1573376 | tf_op jit(solution)/shard_map/scatter-add | solution.py:59
  237.1 3.1 copy.50
  240.2 4.3 %fusion.56 = f32[4096,256]{1,0:T(8,128)} fusion(bf16[4096,256]{1,0:T(8,128)(2,1)} %copy-done.3, bf16[1824,256]{1,0:T(8,128)(2,1)} %copy-done.10), kind=kOutput, calls=%fused_computation.106 | convolution fusion | flops 536870912 | bytes 6422528 | tf_op jit(solution)/shard_map/dot_general | solution.py:49
  244.5 24.0 %scatter_custom_fusion.1 = f32[1536,256]{1,0:T(8,128)} fusion(s32[4096]{0:T(1024)S(1)} %get-tuple-element.87, f32[4096,256]{1,0:T(8,128)} %fusion.56, f32[]{:T(128)} %constant.42.clone.1), kind=kCustom, calls=%fused_computation.55 | custom fusion | flops 1048576 | bytes 1573376 | tf_op jit(solution)/shard_map/scatter-add | solution.py:59
  268.5 3.0 copy.49
  271.6 12.9 %all-reduce.4.cloned.1.call-done = f32[1824,256]{1,0:T(8,128)} async-done(((f32[1824,256]{1,0:T(8,128)}), f32[1824,256]{1,0:T(8,128)}) %all-reduce.4.cloned.1.call-update) | async-done | bytes 1867792 | tf_op jit(solution)/shard_map/psum | solution.py:217
  284.5 3.3 fusion.78
  287.9 0.8 fusion.80
  288.7 2.6 collective-permute-start.7
  292.7 1.0 copy.51
  293.7 3.7 fusion.5
  297.9 3.8 %collective-permute-done.7 = bf16[512,256]{0,1:T(8,128)(2,1)} collective-permute-done((bf16[512,256]{0,1:T(8,128)(2,1)}, bf16[512,256]{0,1:T(8,128)(2,1)}, u32[]{:S(2)}, u32[]{:S(2)}) %collective-permute-start.7) | collective-permute-done | bytes 262176 | tf_op jit(solution)/shard_map/ppermute | solution.py:35
  301.7 1.4 fusion.30
  303.1 46.0 %all-reduce.6.cloned.1.call-done = f32[1824,256]{1,0:T(8,128)} async-done(((f32[1824,256]{1,0:T(8,128)}), f32[1824,256]{1,0:T(8,128)}) %all-reduce.6.cloned.1.call-update) | async-done | bytes 1867792 | tf_op jit(solution)/shard_map/psum | solution.py:218
  349.2 1.7 multiply_reduce_fusion.4
  350.9 1.9 fusion.38
  352.8 1.0 copy.52
  353.8 12.6 %all-reduce = (f32[]{:T(128)}, f32[8,256]{1,0:T(8,128)S(1)}) all-reduce(f32[]{:T(128)} %multiply_reduce_fusion.4, f32[8,256]{1,0:T(8,128)} %fusion.38), channel_id=1, replica_groups=mesh['edge'=8,'feat'=4] {'feat'}, use_global_device_ids=true, to_apply=%region_22.24 | all-reduce | flops 2049 | bytes 16392 | tf_op jit(solution)/shard_map/psum | solution.py:226
  367.8 2.8 multiply_add_fusion.1
  (85 shorter events, 7.9 us)
Async XLA Ops:
  7.2 71.8 %copy-start = (bf16[1,4096,256]{2,1,0:T(8,128)(2,1)S(1)}, bf16[1,4096,256]{2,1,0:T(8,128)(2,1)}, u32[]{:S(2)}) copy-start(bf16[1,4096,256]{2,1,0:T(8,128)(2,1)} %param.15) | copy-start | bytes 6291460
  7.2 277.3 %all-reduce.4.cloned.1.call-start = ((), (), s32[]{:S(2)}) async-start(), calls=%async_computation | async-start | bytes 3735552 | tf_op jit(solution)/shard_map/psum | solution.py:217
  8.5 28.5 %copy-start.14 = (bf16[1,512,256]{1,2,0:T(8,128)(2,1)}, bf16[1,512,256]{1,2,0:T(8,128)(2,1)S(1)}, u32[]{:S(2)}) copy-start(bf16[1,512,256]{1,2,0:T(8,128)(2,1)S(1)} %copy.42) | copy-start | bytes 786436
  8.5 28.5 %collective-permute-start = (bf16[512,256]{0,1:T(8,128)(2,1)S(1)}, bf16[512,256]{0,1:T(8,128)(2,1)S(1)}, u32[]{:S(2)}, u32[]{:S(2)}) collective-permute-start(bf16[512,256]{0,1:T(8,128)(2,1)S(1)} %bitcast.84), channel_id=1, source_target_pairs={{0,4},{4,8},{8,12},{12,16},{16,20},{20,24},{24,28},{28,0},{1,5},{5... | collective-permute-start | bytes 786440 | tf_op jit(solution)/shard_map/ppermute | solution.py:23
  9.0 28.0 %collective-permute-start.1 = (bf16[512,256]{0,1:T(8,128)(2,1)S(1)}, bf16[512,256]{0,1:T(8,128)(2,1)S(1)}, u32[]{:S(2)}, u32[]{:S(2)}) collective-permute-start(bf16[512,256]{0,1:T(8,128)(2,1)S(1)} %bitcast.85), channel_id=1, source_target_pairs={{4,0},{8,4},{12,8},{16,12},{20,16},{24,20},{28,24},{0,28},{5,1},{9... | collective-permute-start | bytes 786440 | tf_op jit(solution)/shard_map/ppermute | solution.py:25
  36.0 0.9 copy-start.10
  73.3 4.0 %copy-start.8 = (bf16[4096,256]{1,0:T(8,128)(2,1)S(1)}, bf16[4096,256]{1,0:T(8,128)(2,1)}, u32[]{:S(2)}) copy-start(bf16[4096,256]{1,0:T(8,128)(2,1)} %gather_fusion.1) | copy-start | bytes 6291460
  79.0 1.7 copy-start.23
  84.7 1.8 copy-start.6
  86.5 2.0 copy-start.1
  96.8 30.2 %copy-start.24 = (s32[512]{0:T(512)S(1)}, s32[512]{0:T(512)}, u32[]{:S(2)}) copy-start(s32[512]{0:T(512)} %param.19) | copy-start | bytes 6148
  96.8 30.2 %copy-start.13 = (bf16[1,512,256]{2,1,0:T(8,128)(2,1)S(1)}, bf16[1,512,256]{2,1,0:T(8,128)(2,1)}, u32[]{:S(2)}) copy-start(bf16[1,512,256]{2,1,0:T(8,128)(2,1)} %param.14) | copy-start | bytes 786436
  123.2 14.4 %collective-permute-start.2 = (f32[512,256]{1,0:T(8,128)}, f32[512,256]{1,0:T(8,128)S(1)}, u32[]{:S(2)}, u32[]{:S(2)}) collective-permute-start(f32[512,256]{1,0:T(8,128)} %get-tuple-element.61), channel_id=1, source_target_pairs={{0,4},{4,8},{8,12},{12,16},{16,20},{20,24},{24,28},{28,0},{1,5},{5... | collective-permute-start | bytes 1572872 | tf_op jit(solution)/shard_map/ppermute | solution.py:35
  123.2 15.2 %collective-permute-start.3 = (f32[512,256]{1,0:T(8,128)}, f32[512,256]{1,0:T(8,128)}, u32[]{:S(2)}, u32[]{:S(2)}) collective-permute-start(f32[512,256]{1,0:T(8,128)} %get-tuple-element.62), channel_id=1, source_target_pairs={{0,28},{4,0},{8,4},{12,8},{16,12},{20,16},{24,20},{28,24},{1,29},{... | collective-permute-start | bytes 1572872 | tf_op jit(solution)/shard_map/ppermute | solution.py:35
  137.6 0.8 copy-start.21
  139.8 2.9 copy-start.15
  146.1 10.4 %copy-start.11 = (bf16[512,256]{1,0:T(8,128)(2,1)}, bf16[512,256]{1,0:T(8,128)(2,1)S(1)}, u32[]{:S(2)}) copy-start(bf16[512,256]{1,0:T(8,128)(2,1)S(1)} %get-tuple-element.85) | copy-start | bytes 786436
  147.3 9.2 %collective-permute-start.4 = (bf16[512,256]{1,0:T(8,128)(2,1)S(1)}, bf16[512,256]{1,0:T(8,128)(2,1)S(1)}, u32[]{:S(2)}, u32[]{:S(2)}) collective-permute-start(bf16[512,256]{1,0:T(8,128)(2,1)S(1)} %convolution_convert_fusion.1), channel_id=1, source_target_pairs={{0,4},{4,8},{8,12},{12,16},{16,20},{20,24},{24,28},{28,0},{1,5},{5... | collective-permute-start | bytes 786440 | tf_op jit(solution)/shard_map/ppermute | solution.py:23
  147.4 9.1 %collective-permute-start.5 = (bf16[512,256]{1,0:T(8,128)(2,1)S(1)}, bf16[512,256]{1,0:T(8,128)(2,1)S(1)}, u32[]{:S(2)}, u32[]{:S(2)}) collective-permute-start(bf16[512,256]{1,0:T(8,128)(2,1)S(1)} %convolution_convert_fusion.1), channel_id=1, source_target_pairs={{4,0},{8,4},{12,8},{16,12},{20,16},{24,20},{28,24},{0,28},{5,1},{9... | collective-permute-start | bytes 786440 | tf_op jit(solution)/shard_map/ppermute | solution.py:25
  177.6 5.4 %copy-start.2 = (f32[4096,256]{0,1:T(8,128)S(1)}, f32[4096,256]{0,1:T(8,128)}, u32[]{:S(2)}) copy-start(f32[4096,256]{0,1:T(8,128)} %copy-done.1) | copy-start | bytes 12582916
  177.6 5.4 %copy-start.4 = (bf16[4096,256]{0,1:T(8,128)(2,1)S(1)}, bf16[4096,256]{0,1:T(8,128)(2,1)}, u32[]{:S(2)}) copy-start(bf16[4096,256]{0,1:T(8,128)(2,1)} %copy.48) | copy-start | bytes 6291460
  183.0 2.3 copy-start.7
  185.3 2.3 copy-start.25
  187.6 3.0 copy-start.5
  190.6 6.2 %copy-start.3 = (bf16[4096,256]{1,0:T(8,128)(2,1)}, bf16[4096,256]{1,0:T(8,128)(2,1)S(1)}, u32[]{:S(2)}) copy-start(bf16[4096,256]{1,0:T(8,128)(2,1)S(1)} %get-tuple-element.83) | copy-start | bytes 6291460
  190.6 2.3 copy-start.9
  196.8 1.0 copy-start.18
  196.8 1.0 copy-start.19
  196.8 1.1 copy-start.20
  207.9 141.2 %all-reduce.6.cloned.1.call-start = ((), (), s32[]{:S(2)}) async-start(), calls=%async_computation.1 | async-start | bytes 3735552 | tf_op jit(solution)/shard_map/psum | solution.py:218
  284.5 8.2 %copy-start.16 = (f32[1,512,256]{1,2,0:T(8,128)S(1)}, f32[1,512,256]{1,2,0:T(8,128)}, u32[]{:S(2)}) copy-start(f32[1,512,256]{1,2,0:T(8,128)} %get-tuple-element.65) | copy-start | bytes 1572868
  288.7 9.2 %collective-permute-start.6 = (bf16[512,256]{0,1:T(8,128)(2,1)}, bf16[512,256]{0,1:T(8,128)(2,1)S(1)}, u32[]{:S(2)}, u32[]{:S(2)}) collective-permute-start(bf16[512,256]{0,1:T(8,128)(2,1)} %get-tuple-element.63), channel_id=1, source_target_pairs={{0,4},{4,8},{8,12},{12,16},{16,20},{20,24},{24,28},{28,0},{1,5},{5... | collective-permute-start | bytes 786440 | tf_op jit(solution)/shard_map/ppermute | solution.py:35
  288.7 13.0 %collective-permute-start.7 = (bf16[512,256]{0,1:T(8,128)(2,1)}, bf16[512,256]{0,1:T(8,128)(2,1)}, u32[]{:S(2)}, u32[]{:S(2)}) collective-permute-start(bf16[512,256]{0,1:T(8,128)(2,1)} %get-tuple-element.64), channel_id=1, source_target_pairs={{0,28},{4,0},{8,4},{12,8},{16,12},{20,16},{24,20},{28,24},{1,29},{... | collective-permute-start | bytes 786440 | tf_op jit(solution)/shard_map/ppermute | solution.py:35
  293.7 8.0 %copy-start.12 = (bf16[512,256]{1,0:T(8,128)(2,1)S(1)}, bf16[512,256]{1,0:T(8,128)(2,1)}, u32[]{:S(2)}) copy-start(bf16[512,256]{1,0:T(8,128)(2,1)} %copy-done.11) | copy-start | bytes 786436
  303.1 64.7 %copy-start.17 = (f32[456,256]{1,0:T(8,128)S(1)}, f32[456,256]{1,0:T(8,128)}, u32[]{:S(2)}) copy-start(f32[456,256]{1,0:T(8,128)} %param.20) | copy-start | bytes 1400836
  303.1 64.7 %copy-start.22 = (f32[456,256]{1,0:T(8,128)S(1)}, f32[456,256]{1,0:T(8,128)}, u32[]{:S(2)}) copy-start(f32[456,256]{1,0:T(8,128)} %param.23) | copy-start | bytes 1400836
Sparse Core Ops, SparseCore 0:
  208.1 76.3 all-reduce.3
  287.8 61.2 all-reduce.5
